TPU v7x, 128 devices: a whole 4x4x4 slice. The times are simulated.
128 devices in a mesh: gx: 8 (over z_lo, x), gy: 4 (over z_hi, core), gz: 4 (over y).
Axes of the slice: x: 4, y: 4, z: 4 (z_hi: 2, z_lo: 2; z = z_hi * 2 + z_lo), core: 2. Of those that a mesh axis runs over, the one named last changes fastest.
Arguments:
- x_saved: bfloat16 [1024, 16384], P('gx', ('gy', 'gz')), may hold values from -0.1875 to 0.1875
- grad_out: bfloat16 [1024, 28672], P('gx', ('gz', 'gy')), may hold values from -6 to 6
- weight: bfloat16 [16384, 28672], P('gy', ('gz', 'gx')), may hold values from -0.09375 to 0.09375
Outputs:
- grad_in: bfloat16 [1024, 16384], P('gx', ('gy', 'gz'))
- grad_weight: bfloat16 [16384, 28672], P('gy', ('gz', 'gx'))
All inputs are finite; a program needn't handle non-finite values.
Results may differ from a plain program's by a relative error of at most 0.001.
Values may be sent and summed in bfloat16 or wider, within the bound.
A program may use at most 128 MiB of HBM per device.

v0:
```python
import jax
import jax.numpy as jnp
from jax import lax
from jax.sharding import PartitionSpec as P


def body(x_saved, grad_out, weight):
    token_rows = x_saved.shape[0]
    token_groups = lax.axis_size("gx")
    feature_groups = lax.axis_size("gz")
    grad_block = lax.all_gather(grad_out, "gy", axis=1, tiled=True)
    grad_all = lax.all_to_all(grad_block, "gx", split_axis=1, concat_axis=0, tiled=True)
    unit_cols = grad_all.shape[1]
    inputs_block = lax.all_gather(x_saved, "gz", axis=1, tiled=True)
    summed = jnp.einsum(
        "td,tc->dc",
        lax.all_gather(inputs_block, "gx", axis=0, tiled=True),
        grad_all,
        preferred_element_type=jnp.float32,
    )
    grad_weight = summed.astype(jnp.bfloat16)
    grad_split = grad_all.reshape(token_groups, token_rows, unit_cols)
    weight_split = weight.reshape(feature_groups, weight.shape[0] // feature_groups, unit_cols)
    terms = jnp.einsum(
        "atc,bkc->abtk", grad_split, weight_split, preferred_element_type=jnp.float32
    )
    terms = terms.reshape(token_groups * feature_groups * token_rows, weight_split.shape[1])
    grad_in = lax.psum_scatter(terms, ("gx", "gz"), scatter_dimension=0, tiled=True)
    return (grad_in.astype(jnp.bfloat16), grad_weight)


def solution(mesh):
    return jax.shard_map(
        body,
        mesh=mesh,
        in_specs=(P("gx", ("gy", "gz")), P("gx", ("gz", "gy")), P("gy", ("gz", "gx"))),
        out_specs=(P("gx", ("gy", "gz")), P("gy", ("gz", "gx"))),
        check_vma=False,
    )
```

profile of v0, /device:TPU:0, one launch (start us, length us, event | category | flops | bytes accessed | tf_op | source)
XLA Modules:
  0.0 388.2 jit_solution(9099532467425328987)
XLA Ops:
  7.2 0.0 all-gather.6.cloned.1.call-start
  7.2 0.7 all-gather.6.cloned.1.call-update
  7.9 0.0 all-gather.4.cloned.1.call-start
  7.9 2.0 copy.5
  9.9 0.0 all-gather.4.cloned.1.call-update
  10.0 0.0 all-gather.8.cloned.1.call-start
  10.0 26.3 %all-gather.6.cloned.1.call-done = bf16[128,4096]{1,0:T(8,128)(2,1)} async-done(((bf16[128,1024]{1,0:T(8,128)(2,1)}), bf16[128,4096]{1,0:T(8,128)(2,1)}) %all-gather.6.cloned.1.call-update) | async-done | bytes 1048592 | tf_op jit(solution)/shard_map/all_gather | solution.py:14
  36.3 0.0 all-gather.8.cloned.1.call-update
  36.3 0.0 reduce-scatter.2.cloned.1.call-start
  36.3 27.8 %all-gather.4.cloned.1.call-done = bf16[128,7168]{0,1:T(8,128)(2,1)} async-done(((bf16[128,1792]{0,1:T(8,128)(2,1)}), bf16[128,7168]{0,1:T(8,128)(2,1)}) %all-gather.4.cloned.1.call-update) | async-done | bytes 1835024 | tf_op jit(solution)/shard_map/all_gather | solution.py:11
  64.2 3.1 copy.6
  67.2 46.0 %all_to_all.19 = bf16[128,8,896]{2,0,1:T(8,128)(2,1)S(1)} all-to-all(bf16[128,8,896]{2,0,1:T(8,128)(2,1)S(1)} %copy.6), channel_id=1, replica_groups=mesh['gx'=8,'gy'=4,'gz'=4] {'gx'}, dimensions={1} | all-to-all | bytes 3670016 | tf_op jit(solution)/shard_map/all_to_all | solution.py:12
  113.3 0.0 copy-start
  113.3 11.8 %convolution_bitcast_fusion = f32[8,4,128,1024]{3,2,0,1:T(8,128)S(1)} fusion(bf16[4,1024,896,1]{2,1,3,0:T(8,128)(2,1)} %bitcast.22, bf16[128,8,896]{2,0,1:T(8,128)(2,1)S(1)} %all_to_all.19), kind=kOutput, calls=%fused_computation | convolution fusion | flops 7516192768 | bytes 25952256 | tf_op jit(solution)/shard_map/atc,bkc->abtk/dot_general | solution.py:24
  125.1 0.0 copy-done
  125.1 6.1 %copy.7 = f32[8,4,128,1024]{3,2,1,0:T(8,128)} copy(f32[8,4,128,1024]{3,2,0,1:T(8,128)S(1)} %convolution_bitcast_fusion) | data formatting | bytes 33554432 | tf_op jit(solution)/shard_map/atc,bkc->abtk/transpose | solution.py:24
  131.2 0.0 copy-start.1
  131.2 0.0 reduce-scatter.2.cloned.1.call-update
  131.2 43.9 %all-gather.8.cloned.1.call-done = bf16[1024,4096]{1,0:T(8,128)(2,1)} async-done(((bf16[128,4096]{1,0:T(8,128)(2,1)}), bf16[1024,4096]{1,0:T(8,128)(2,1)}) %all-gather.8.cloned.1.call-update) | async-done | bytes 8388624 | tf_op jit(solution)/shard_map/all_gather | solution.py:17
  175.1 0.0 copy-done.1
  175.1 14.2 %convolution_convert_fusion = bf16[4096,896]{1,0:T(8,128)(2,1)} fusion(bf16[1024,4096]{1,0:T(8,128)(2,1)} %all-gather.8.cloned.1.call-done, bf16[1024,896]{1,0:T(8,128)(2,1)S(1)} %bitcast.21), kind=kOutput, calls=%fused_computation.1 | convolution fusion | flops 7519862784 | bytes 17563648 | tf_op jit(solution)/shard_map/td,tc->dc/dot_general | solution.py:15
  189.4 190.5 %reduce-scatter.2.cloned.1.call-done = f32[128,1024]{1,0:T(8,128)} async-done(((f32[4096,1024]{1,0:T(8,128)}), f32[128,1024]{1,0:T(8,128)}) %reduce-scatter.2.cloned.1.call-update) | async-done | bytes 524304 | tf_op jit(solution)/shard_map/reduce_scatter | solution.py:28
  379.9 1.8 convert_element_type.6
Async XLA Ops:
  7.2 29.1 %all-gather.6.cloned.1.call-start = ((), (), s32[]{:S(2)}) async-start(), calls=%async_computation.4 | async-start | bytes 1310720 | tf_op jit(solution)/shard_map/all_gather | solution.py:14
  7.9 56.3 %all-gather.4.cloned.1.call-start = ((), (), s32[]{:S(2)}) async-start(), calls=%async_computation.2 | async-start | bytes 2293760 | tf_op jit(solution)/shard_map/all_gather | solution.py:11
  10.0 165.2 %all-gather.8.cloned.1.call-start = ((), (), s32[]{:S(2)}) async-start(), calls=%async_computation.5 | async-start | bytes 9437184 | tf_op jit(solution)/shard_map/all_gather | solution.py:17
  36.3 343.6 %reduce-scatter.2.cloned.1.call-start = ((), (), s32[]{:S(2)}) async-start(), calls=%async_computation.3 | async-start | bytes 17301504 | tf_op jit(solution)/shard_map/reduce_scatter | solution.py:28
  113.3 11.8 %copy-start = (bf16[128,8,896]{2,0,1:T(8,128)(2,1)}, bf16[128,8,896]{2,0,1:T(8,128)(2,1)S(1)}, u32[]{:S(2)}) copy-start(bf16[128,8,896]{2,0,1:T(8,128)(2,1)S(1)} %all_to_all.19) | copy-start | bytes 5505028
  131.2 43.9 %copy-start.1 = (bf16[128,8,896]{2,0,1:T(8,128)(2,1)S(1)}, bf16[128,8,896]{2,0,1:T(8,128)(2,1)}, u32[]{:S(2)}) copy-start(bf16[128,8,896]{2,0,1:T(8,128)(2,1)} %copy-done) | copy-start | bytes 5505028
Sparse Core Ops, SparseCore 0:
  9.6 26.5 all-gather.5
  38.5 25.6 all-gather.3
  65.8 109.2 all-gather.7
  177.4 202.4 reduce-scatter.1
where the time goes:
time: 389 us; the launch traced here: 388 us
  waiting for transfers between devices  289 us (74%)
  blocking collectives  46 us (12%)
  matrix products  26 us (7%)
  between operations  13.8 us (4%)
  local copies, waits for them, and re-layouts  11.2 us (3%)
    reduce_scatter x1, waiting for transfers between devices, body(): lax.psum_scatter(terms, ('gx', 'gz'), scatter_dimension=0, tiled=True)  191 us
    all_to_all x1, blocking collectives, body(): lax.all_to_all(grad_block, 'gx', split_axis=1, concat_axis=0, tiled=True)  46 us
    all_gather x1, waiting for transfers between devices, body(): lax.all_gather(inputs_block, 'gx', axis=0, tiled=True)  43.9 us
    all_gather x1, waiting for transfers between devices, body(): grad_block = lax.all_gather(grad_out, 'gy', axis=1, tiled=True)  27.8 us
    all_gather x1, waiting for transfers between devices, body(): inputs_block = lax.all_gather(x_saved, 'gz', axis=1, tiled=True)  26.3 us
    dot_general x1, matrix products, body(): jnp.einsum('td,tc->dc', lax.all_gather(inputs_block, 'gx', axis=0, tiled=...  14.2 us
    dot_general x1, matrix products, body(): jnp.einsum('atc,bkc->abtk', grad_split, weight_split, preferred_element_t...  11.8 us
  transfers between devices with their start and end apart: 4, of which 4 were waited for; matrix products, arithmetic and copies ran while one was open for 10% of the time, Pallas kernels for 0%

commit v1 on v0

v1 whole, which is shorter than its diff:
```python
import jax
import jax.numpy as jnp
from jax import lax
from jax.experimental import pallas as pl
from jax.experimental.pallas import tpu as pltpu
from jax.sharding import PartitionSpec as P

MESH = pl.DeviceIdType.MESH
NX, NY, NZ = 4, 4, 2
ROWS = 128
TILE = 256
STREAMS = ((0, 1), (0, -1), (1, 1), (1, -1))


def kernel(
    grad_ref, weight_hbm, grad_in_ref, grad_all_hbm,
    grad_all, weight, send1, recv1, send2, recv2, send3, recv3,
    gather_send, gather_recv, weight_sem, out_sem,
    s1_sem, r1_sem, s2_sem, r2_sem, s3_sem, r3_sem,
):
    gx, gy, gz = lax.axis_index("gx"), lax.axis_index("gy"), lax.axis_index("gz")
    z, x, y = gx // NX, gx % NX, gz
    cols = weight.shape[1]
    width = weight.shape[0] // NY

    load = pltpu.make_async_copy(weight_hbm, weight, weight_sem)
    load.start()

    barrier = pltpu.get_barrier_semaphore()
    for a in range(8):
        for b in range(4):
            @pl.when(jnp.logical_or(gx != a, gy != b))
            def _():
                pl.semaphore_signal(
                    barrier, inc=1, device_id={"gx": a, "gy": b, "gz": gz}, device_id_type=MESH
                )
    for d in (1, NY - 1):
        pl.semaphore_signal(
            barrier, inc=1, device_id={"gx": gx, "gy": gy, "gz": (gz + d) % NY}, device_id_type=MESH
        )
    pl.semaphore_wait(barrier, 33)

    def row_of(s):
        return pl.ds(pl.multiple_of(((s % NX) * NZ + s // NX) * ROWS, ROWS), ROWS)

    def gather_copy(h, b):
        return pltpu.make_async_remote_copy(
            src_ref=grad_ref.at[:, pl.ds(h * cols, cols)],
            dst_ref=grad_all.at[row_of(gx)],
            send_sem=gather_send.at[h * 4 + b],
            recv_sem=gather_recv.at[gx],
            device_id={"gx": 2 * gy + h, "gy": b, "gz": gz},
            device_id_type=MESH,
        )

    def is_self(h, b):
        return jnp.logical_and(gx == 2 * gy + h, gy == b)

    for h in range(2):
        for b in range(4):
            @pl.when(jnp.logical_not(is_self(h, b)))
            def _():
                gather_copy(h, b).start()

            @pl.when(is_self(h, b))
            def _():
                pltpu.make_async_copy(
                    grad_ref.at[:, pl.ds(h * cols, cols)],
                    grad_all.at[row_of(gx)],
                    gather_recv.at[gx],
                ).start()
    for s in range(8):
        pltpu.make_async_copy(
            grad_ref.at[:, pl.ds(0, cols)], grad_all.at[row_of(s)], gather_recv.at[s]
        ).wait()
    load.wait()

    def out_copy(s):
        return pltpu.make_async_copy(
            grad_all.at[row_of(s)], grad_all_hbm.at[pl.ds(s * ROWS, ROWS)], out_sem.at[s]
        )

    for s in range(8):
        out_copy(s).start()

    def term(n, tx, ty):
        units = grad_all[pl.ds(pl.multiple_of(tx * NZ * ROWS, NZ * ROWS), NZ * ROWS), :]
        feats = weight[pl.ds(pl.multiple_of(ty * width + n * TILE, TILE), TILE), :]
        return lax.dot_general(
            units, feats, (((1,), (1,)), ((), ())), preferred_element_type=jnp.float32
        )

    def neighbour(along, sign):
        if along == 0:
            return {"gx": z * NX + (x + sign + NX) % NX, "gy": gy, "gz": gz}
        return {"gx": gx, "gy": gy, "gz": (y + sign + NY) % NY}

    def copy1(n, s, q):
        along, sign = STREAMS[n]
        return pltpu.make_async_remote_copy(
            src_ref=send1.at[n, s, q], dst_ref=recv1.at[n, s, q],
            send_sem=s1_sem.at[n, s, q], recv_sem=r1_sem.at[n, s, q],
            device_id=neighbour(along, sign), device_id_type=MESH,
        )

    def copy2(n, q):
        along, sign = STREAMS[n]
        return pltpu.make_async_remote_copy(
            src_ref=send2.at[n, q], dst_ref=recv2.at[n, q],
            send_sem=s2_sem.at[n, q], recv_sem=r2_sem.at[n, q],
            device_id=neighbour(1 - along, sign), device_id_type=MESH,
        )

    def copy3(n):
        return pltpu.make_async_remote_copy(
            src_ref=send3.at[n, 1 - z], dst_ref=recv3.at[n],
            send_sem=s3_sem.at[n], recv_sem=r3_sem.at[n],
            device_id={"gx": (1 - z) * NX + x, "gy": gy, "gz": gz}, device_id_type=MESH,
        )

    def target(n, s, q):
        along, sign = STREAMS[n]
        if along == 0:
            return (x + 8 - sign * (1 + s)) % NX, (y + 8 - sign * (1 + q)) % NY
        return (x + 8 - sign * (1 + q)) % NX, (y + 8 - sign * (1 + s)) % NY

    for s in range(3):
        @pl.loop(0, 4)
        def _(q):
            for n in range(4):
                value = term(n, *target(n, s, q))
                if s > 0:
                    copy1(n, s - 1, q).wait_recv()
                    value = value + recv1[n, s - 1, q]
                send1[n, s, q] = value
                copy1(n, s, q).start()

    for q in range(4):
        for n in range(4):
            value = term(n, *target(n, 3, q))
            copy1(n, 2, q).wait_recv()
            value = value + recv1[n, 2, q]
            if q > 0:
                copy2(n, q - 1).wait_recv()
                value = value + recv2[n, q - 1]
            if q < 3:
                send2[n, q] = value
                copy2(n, q).start()
            else:
                send3[n, 0] = value[:ROWS]
                send3[n, 1] = value[ROWS:]
                copy3(n).start()

    for n in range(4):
        copy3(n).wait_recv()
        grad_in_ref[:, pl.ds(n * TILE, TILE)] = (send3[n, z] + recv3[n]).astype(grad_in_ref.dtype)

    for s in range(3):
        @pl.loop(0, 4)
        def _(q):
            for n in range(4):
                copy1(n, s, q).wait_send()
    for n in range(4):
        for q in range(3):
            copy2(n, q).wait_send()
        copy3(n).wait_send()
    for h in range(2):
        for b in range(4):
            @pl.when(jnp.logical_not(is_self(h, b)))
            def _():
                gather_copy(h, b).wait_send()
    for s in range(8):
        out_copy(s).wait()


def grad_in_and_units(grad_out, weight):
    features, cols = weight.shape
    tile = (NZ * ROWS, TILE)
    f32 = jnp.float32
    return pl.pallas_call(
        kernel,
        out_shape=(
            jax.ShapeDtypeStruct((ROWS, features // NY), jnp.bfloat16),
            jax.ShapeDtypeStruct((8 * ROWS, cols), jnp.bfloat16),
        ),
        in_specs=[pl.BlockSpec(memory_space=pltpu.VMEM), pl.BlockSpec(memory_space=pl.ANY)],
        out_specs=(pl.BlockSpec(memory_space=pltpu.VMEM), pl.BlockSpec(memory_space=pl.ANY)),
        scratch_shapes=[
            pltpu.VMEM((8 * ROWS, cols), jnp.bfloat16),
            pltpu.VMEM((features, cols), jnp.bfloat16),
            pltpu.VMEM((4, 3, 4) + tile, f32),
            pltpu.VMEM((4, 3, 4) + tile, f32),
            pltpu.VMEM((4, 3) + tile, f32),
            pltpu.VMEM((4, 3) + tile, f32),
            pltpu.VMEM((4, NZ, ROWS, TILE), f32),
            pltpu.VMEM((4, ROWS, TILE), f32),
            pltpu.SemaphoreType.DMA((8,)),
            pltpu.SemaphoreType.DMA((8,)),
            pltpu.SemaphoreType.DMA,
            pltpu.SemaphoreType.DMA((8,)),
            pltpu.SemaphoreType.DMA((4, 3, 4)),
            pltpu.SemaphoreType.DMA((4, 3, 4)),
            pltpu.SemaphoreType.DMA((4, 3)),
            pltpu.SemaphoreType.DMA((4, 3)),
            pltpu.SemaphoreType.DMA((4,)),
            pltpu.SemaphoreType.DMA((4,)),
        ],
        compiler_params=pltpu.CompilerParams(
            collective_id=0, has_side_effects=True, vmem_limit_bytes=52 * 2**20
        ),
        cost_estimate=pl.CostEstimate(
            flops=10**11, bytes_accessed=10**7, transcendentals=0
        ),
    )(grad_out, weight)


def body(x_saved, grad_out, weight):
    grad_in, grad_all = grad_in_and_units(grad_out, weight)
    inputs_block = lax.all_gather(x_saved, "gz", axis=1, tiled=True)
    summed = jnp.einsum(
        "td,tc->dc",
        lax.all_gather(inputs_block, "gx", axis=0, tiled=True),
        grad_all,
        preferred_element_type=jnp.float32,
    )
    return (grad_in, summed.astype(jnp.bfloat16))


def solution(mesh):
    return jax.shard_map(
        body,
        mesh=mesh,
        in_specs=(P("gx", ("gy", "gz")), P("gx", ("gz", "gy")), P("gy", ("gz", "gx"))),
        out_specs=(P("gx", ("gy", "gz")), P("gy", ("gz", "gx"))),
        check_vma=False,
    )
```

time: 389 us -> 284 us (0.73)
  waiting for transfers between devices: 289 us -> 29 us
  Pallas kernels: 0 us -> 211 us
  blocking collectives: 46 us -> 0 us
  matrix products: 26 us -> 12.6 us
    pallas_call x0 -> x1, Pallas kernels: none -> 211 us  [grad_in_and_units(): pl.pallas_call(kernel, out_shape=(jax.ShapeDtypeStruct((ROWS, features //...]
    reduce_scatter x1 -> x0, waiting for transfers between devices: 191 us -> none  [body(): lax.psum_scatter(terms, ('gx', 'gz'), scatter_dimension=0, tiled=True)]
    all_to_all x1 -> x0, blocking collectives: 46 us -> none  [body(): lax.all_to_all(grad_block, 'gx', split_axis=1, concat_axis=0, tiled=True)]
    all_gather x1, waiting for transfers between devices: 43.9 us -> 0.02 us  [body(): lax.all_gather(inputs_block, 'gx', axis=0, tiled=True)]
    all_gather x1 -> x0, waiting for transfers between devices: 27.8 us -> none  [body(): grad_block = lax.all_gather(grad_out, 'gy', axis=1, tiled=True)]
    dot_general x1 -> x0, matrix products: 11.8 us -> none  [body(): jnp.einsum('atc,bkc->abtk', grad_split, weight_split, preferred_element_t...]
    unnamed x5 -> x4, local copies, waits for them, and re-layouts: 2 us -> 12.5 us
    transpose x1 -> x0, local copies, waits for them, and re-layouts: 6.11 us -> none  [body(): jnp.einsum('atc,bkc->abtk', grad_split, weight_split, preferred_element_t...]
  transfers between devices with their start and end apart: 4 -> 2, of which waited for: 4 -> 1; matrix products, arithmetic and copies ran while one was open for 10% -> 0% of each run, Pallas kernels for 0% -> 76%
where the time goes in v1:
time: 284 us; the launch traced here: 279 us
  Pallas kernels  211 us (74%)
  waiting for transfers between devices  29 us (10%)
  between operations  14.1 us (5%)
  matrix products  12.6 us (4%)
  local copies, waits for them, and re-layouts  12.5 us (4%)
    pallas_call x1, Pallas kernels, grad_in_and_units(): pl.pallas_call(kernel, out_shape=(jax.ShapeDtypeStruct((ROWS, features //...  211 us
    all_gather x1, waiting for transfers between devices, body(): inputs_block = lax.all_gather(x_saved, 'gz', axis=1, tiled=True)  28.3 us
    dot_general x1, matrix products, body(): jnp.einsum('td,tc->dc', lax.all_gather(inputs_block, 'gx', axis=0, tiled=...  12.6 us
    unnamed x4, local copies, waits for them, and re-layouts  12.5 us
  transfers between devices with their start and end apart: 2, of which 1 were waited for; matrix products, arithmetic and copies ran while one was open for 0% of the time, Pallas kernels for 76%

profile of v1, /device:TPU:0, one launch (start us, length us, event | category | flops | bytes accessed | tf_op | source)
XLA Modules:
  0.0 279.4 jit_solution(17908850987213515377)
XLA Ops:
  7.2 0.0 all-gather.3.cloned.1.call-start
  7.2 0.7 all-gather.3.cloned.1.call-update
  7.9 0.0 all-gather.5.cloned.1.call-start
  7.9 28.3 %all-gather.3.cloned.1.call-done = bf16[128,4096]{1,0:T(8,128)(2,1)} async-done(((bf16[128,1024]{1,0:T(8,128)(2,1)}), bf16[128,4096]{1,0:T(8,128)(2,1)}) %all-gather.3.cloned.1.call-update) | async-done | bytes 1048592 | tf_op jit(solution)/shard_map/all_gather | solution.py:219
  36.3 0.0 all-gather.5.cloned.1.call-update
  36.3 0.0 copy-start
  36.3 1.0 copy-done
  37.3 211.0 %shard_map.50 = (bf16[128,1024]{1,0:T(8,128)(2,1)S(1)}, bf16[1024,896]{1,0:T(8,128)(2,1)}) custom-call(bf16[128,1792]{1,0:T(8,128)(2,1)S(1)} %copy-done, bf16[4096,896]{1,0:T(8,128)(2,1)} %weight_hbm.1), custom_call_target="tpu_custom_call" | custom-call | flops 99999997952 | bytes 10000000 | tf_op jit(solution)/shard_map/pallas_call | solution.py:180
  248.4 0.0 all-gather.5.cloned.1.call-done
  248.4 12.6 %convert_bitcast_fusion = bf16[4096,896]{0,1:T(8,128)(2,1)} fusion(bf16[1024,896]{1,0:T(8,128)(2,1)} %get-tuple-element.5, bf16[1024,4096]{1,0:T(8,128)(2,1)} %all-gather.5.cloned.1.call-done), kind=kOutput, calls=%fused_computation | convolution fusion | flops 7519862784 | bytes 17563648 | tf_op jit(solution)/shard_map/td,tc->dc/dot_general | solution.py:220
  261.0 10.8 %copy.5 = bf16[4096,896]{1,0:T(8,128)(2,1)} copy(bf16[4096,896]{0,1:T(8,128)(2,1)} %convert_bitcast_fusion) | data formatting | bytes 14680064
  271.8 0.7 copy.7
Async XLA Ops:
  7.2 29.1 %all-gather.3.cloned.1.call-start = ((), (), s32[]{:S(2)}) async-start(), calls=%async_computation | async-start | bytes 1310720 | tf_op jit(solution)/shard_map/all_gather | solution.py:219
  7.9 240.5 %all-gather.5.cloned.1.call-start = ((), (), s32[]{:S(2)}) async-start(), calls=%async_computation.1 | async-start | bytes 9437184 | tf_op jit(solution)/shard_map/all_gather | solution.py:222
  36.3 1.0 copy-start
Sparse Core Ops, SparseCore 0:
  9.6 26.5 all-gather.2
  37.9 175.7 all-gather.4
